TPU v7x, 256 devices: a whole 4x4x8 slice. The times are simulated.
256 devices in a mesh: req: 32 (over z, y), mdl: 8 (over x, core).
Axes of the slice: x: 4, y: 4, z: 8, core: 2. Of those that a mesh axis runs over, the one named last changes fastest.
Arguments:
- stream: bfloat16 [24576, 1792], P('req'), may hold values from -6 to 6
- attention_projection_weight: bfloat16 [3, 1792, 1792], P(None, 'mdl'), may hold values from -0.125 to 0.125
- head_output_weight: bfloat16 [1792, 1792], P('mdl'), may hold values from -0.125 to 0.125
- adapter_down_maps: bfloat16 [64, 1792, 16], P('mdl'), may hold values from -0.125 to 0.125
- adapter_up_maps: bfloat16 [2, 1792, 1024], P(None, 'mdl'), may hold values from -1.5 to 1.5
- tenant_adapter_scale: float32 [4], replicated, may hold values from 0.5 to 2
- feedforward_norm_gain: bfloat16 [1792], replicated, may hold values from 0.099609375 to 1.8984375
- feedforward_weight: bfloat16 [3, 1792, 4864], P(None, 'req', 'mdl'), may hold values from -0.125 to 0.125
- prefix_cache_store: bfloat16 [1024, 2, 1792, 128], P('req', None, 'mdl'), may hold values from -140 to 140
- token_adapter_index: int32 [24576], P('req'), may hold values from 0 to 63
- request_token_lengths: int32 [32, 24], P('req'), may hold values from 1 to 192, 768 in all within a row
- request_tenant_index: int32 [768], P('req'), may hold values from 0 to 3
- last_page_holder: int32 [768, 1], replicated, may hold values from 0 to 31; in each aligned block of 24 rows (0 to 23, 24 to 47, ...) at most 2 rows name the same one
- holder_page_slot: int32 [768], replicated, may hold values from 0 to 31
- page_filled_rows: int32 [768], replicated, may hold values from 64 to 128
Outputs:
- layer_out: bfloat16 [24576, 1792], P(('req', 'mdl'))
Inputs may be any that keep to these rules, and one draw needn't show every extreme that they name: `last_page_holder`: within the rows of one index of req (aligned blocks of 24 rows) no holder is named more than 2 times, and one holder exactly 2 times in some blocks. `request_token_lengths`: each row sums to 768; its longest request has exactly 192 tokens.
All inputs are finite; a program needn't handle non-finite values.
Results may differ from a plain program's by a relative error of at most 0.025.
Values may be sent and summed in bfloat16 or wider, within the bound.
A program may use at most 128 MiB of HBM per device.

v0:
```python
import math
import jax
import jax.numpy as jnp
from jax import lax
from jax.sharding import PartitionSpec as P

HEAD_SIZE = 112
WINDOW = 64


def per_device(
    stream,
    attention_projection_weight,
    head_output_weight,
    adapter_down_maps,
    adapter_up_maps,
    tenant_adapter_scale,
    feedforward_norm_gain,
    feedforward_weight,
    prefix_cache_store,
    token_adapter_index,
    request_token_lengths,
    request_tenant_index,
    last_page_holder,
    holder_page_slot,
    page_filled_rows,
):
    tok_count, model_width = stream.shape
    head_column_set = attention_projection_weight.shape[1]
    head_local = head_column_set // HEAD_SIZE
    req_per_dev = request_token_lengths.shape[1]
    rank_total_width = adapter_down_maps.shape[2]
    adapter_number = adapter_up_maps.shape[2] // rank_total_width
    req_devices = lax.axis_size("req")
    req_index = lax.axis_index("req")
    mdl_index = lax.axis_index("mdl")
    row_share = tok_count // lax.axis_size("mdl")
    cap_slots = max(2, (req_per_dev + req_devices - 1) // req_devices + 1)
    projected_rows = jnp.einsum(
        "td,kcd->ktc", stream, attention_projection_weight, preferred_element_type=jnp.float32
    )
    all_onehot = (
        token_adapter_index[:, None] == jnp.arange(adapter_number, dtype=jnp.int32)[None, :]
    )
    holder_count = adapter_down_maps.shape[0]
    holder_rank_rows = jnp.einsum(
        "qf,kfn->qkn", stream, adapter_down_maps, preferred_element_type=jnp.float32
    )
    held_onehot = (
        token_adapter_index[:, None]
        == (mdl_index * holder_count + jnp.arange(holder_count, dtype=jnp.int32))[None, :]
    )
    rank_part = jnp.sum(holder_rank_rows * held_onehot.astype(jnp.float32)[:, :, None], axis=1)
    rank_feat = lax.psum(rank_part.astype(jnp.bfloat16), "mdl")
    broadcast_result = (
        all_onehot.astype(jnp.bfloat16)[:, :, None] * rank_feat[:, None, :]
    ).reshape(tok_count, adapter_number * rank_total_width)
    adapter_column_set = jnp.einsum(
        "iu,pdu->ipd", broadcast_result, adapter_up_maps, preferred_element_type=jnp.float32
    )
    positions = jnp.arange(tok_count, dtype=jnp.int32)
    lengths_row = request_token_lengths[0]
    starts = jnp.cumsum(lengths_row) - lengths_row
    member = (positions[:, None] >= starts[None, :]) & (
        positions[:, None] < (starts + lengths_row)[None, :]
    )
    member_int = member.astype(jnp.int32)
    request_of = jnp.sum(member_int * jnp.arange(req_per_dev, dtype=jnp.int32)[None, :], axis=1)
    relative = positions - jnp.sum(member_int * starts[None, :], axis=1)
    tenant_hot = (
        request_tenant_index[:, None]
        == jnp.arange(tenant_adapter_scale.shape[0], dtype=jnp.int32)[None, :]
    ).astype(jnp.float32)
    request_scale = jnp.sum(tenant_hot * tenant_adapter_scale[None, :], axis=1)
    per_token_scale = jnp.sum(member.astype(jnp.float32) * request_scale[None, :], axis=1)[:, None]
    query_rows = (projected_rows[0] + per_token_scale * adapter_column_set[:, 0]).astype(
        jnp.bfloat16
    )
    key_rows = projected_rows[1].astype(jnp.bfloat16)
    value_row_block = (projected_rows[2] + per_token_scale * adapter_column_set[:, 1]).astype(
        jnp.bfloat16
    )
    owner_column = last_page_holder[:, 0]
    owner_table = owner_column.reshape(req_devices, req_per_dev)
    slot_table = holder_page_slot.reshape(req_devices, req_per_dev)
    owned = (owner_table == req_index).astype(jnp.int32)
    owned_rank = jnp.cumsum(owned, axis=1) - 1
    picked = owned[:, None, :] * (
        owned_rank[:, None, :] == jnp.arange(cap_slots, dtype=jnp.int32)[None, :, None]
    ).astype(jnp.int32)
    send_slot = jnp.sum(picked * slot_table[:, None, :], axis=2)
    fill_table = page_filled_rows.reshape(req_devices, req_per_dev)
    send_fill = jnp.sum(picked * fill_table[:, None, :], axis=2)
    my_owner = lax.dynamic_slice_in_dim(owner_column, req_index * req_per_dev, req_per_dev, 0)
    order_ids = jnp.arange(req_per_dev, dtype=jnp.int32)
    earlier = (my_owner[:, None] == my_owner[None, :]) & (order_ids[:, None] > order_ids[None, :])
    flat_pick = my_owner * cap_slots + jnp.sum(earlier.astype(jnp.int32), axis=1)
    page_inner = prefix_cache_store.shape[1:3]
    page_rows = prefix_cache_store.shape[3]
    pages = jnp.take(prefix_cache_store, send_slot.reshape(-1), axis=0, mode="clip")
    window_pick = (
        jnp.arange(page_rows, dtype=jnp.int32)[None, :, None]
        == send_fill.reshape(-1)[:, None, None]
        - WINDOW
        + jnp.arange(WINDOW, dtype=jnp.int32)[None, None, :]
    ).astype(jnp.bfloat16)
    source_pages = jnp.einsum(
        "skcr,srj->sjkc", pages, window_pick, preferred_element_type=jnp.float32
    ).astype(jnp.bfloat16)
    source_pages = source_pages.reshape((req_devices, cap_slots, WINDOW) + page_inner)
    arrived = lax.all_to_all(source_pages, "req", split_axis=0, concat_axis=0, tiled=True)
    prefix = jnp.take(
        arrived.reshape((req_devices * cap_slots, WINDOW) + page_inner),
        flat_pick,
        axis=0,
        mode="clip",
    )
    key_all = jnp.concatenate(
        [key_rows, prefix[:, :, 0].reshape(req_per_dev * WINDOW, head_column_set)], axis=0
    )
    value_all = jnp.concatenate(
        [value_row_block, prefix[:, :, 1].reshape(req_per_dev * WINDOW, head_column_set)], axis=0
    )
    distance = positions[:, None] - positions[None, :]
    local_ok = (request_of[:, None] == request_of[None, :]) & (distance >= 0) & (distance <= WINDOW)
    key_request = jnp.repeat(jnp.arange(req_per_dev, dtype=jnp.int32), WINDOW)
    key_offset = jnp.tile(jnp.arange(WINDOW, dtype=jnp.int32), req_per_dev)
    prefix_ok = (request_of[:, None] == key_request[None, :]) & (
        key_offset[None, :] >= relative[:, None]
    )
    allowed = jnp.concatenate([local_ok, prefix_ok], axis=1)
    query_heads = query_rows.reshape(tok_count, head_local, HEAD_SIZE)
    key_heads = key_all.reshape(-1, head_local, HEAD_SIZE)
    value_heads = value_all.reshape(-1, head_local, HEAD_SIZE)
    scores = jnp.einsum(
        "thd,shd->hts", query_heads, key_heads, preferred_element_type=jnp.float32
    ) * (1.0 / math.sqrt(HEAD_SIZE))
    masked = jnp.where(allowed[None], scores, -1e30)
    row_max = jnp.max(masked, axis=-1, keepdims=True)
    exp_scores = jnp.exp(masked - row_max)
    weights = (exp_scores / jnp.sum(exp_scores, axis=-1, keepdims=True)).astype(jnp.bfloat16)
    mixed = (
        jnp.einsum("hts,shd->thd", weights, value_heads, preferred_element_type=jnp.float32)
        .astype(jnp.bfloat16)
        .reshape(tok_count, head_column_set)
    )
    attn_part = (
        jnp.dot(mixed, head_output_weight, preferred_element_type=jnp.float32)
        .astype(jnp.bfloat16)
        .astype(jnp.float32)
    )
    gain_wide = feedforward_norm_gain.astype(jnp.float32)[None, :]
    attn_full = lax.psum(attn_part.astype(jnp.bfloat16), "mdl").astype(jnp.float32)
    resid_full = (stream.astype(jnp.float32) + attn_full).astype(jnp.bfloat16)
    resid_wide = resid_full.astype(jnp.float32)
    mean_sq = jnp.mean(resid_wide * resid_wide, axis=1, keepdims=True)
    normed = (resid_wide * lax.rsqrt(mean_sq + 1e-06) * gain_wide).astype(jnp.bfloat16)
    resid_mine = lax.dynamic_slice_in_dim(resid_full, mdl_index * row_share, row_share, 0)
    full_mlp = lax.all_gather(feedforward_weight, "req", axis=1, tiled=True)
    gate_part = jnp.dot(normed, full_mlp[0], preferred_element_type=jnp.float32)
    up_part = jnp.dot(normed, full_mlp[1], preferred_element_type=jnp.float32)
    hidden = (jax.nn.silu(gate_part) * up_part).astype(jnp.bfloat16)
    mlp_part = (
        jnp.einsum("tf,df->td", hidden, full_mlp[2], preferred_element_type=jnp.float32)
        .astype(jnp.bfloat16)
        .astype(jnp.float32)
    )
    mlp_mine = lax.psum_scatter(
        mlp_part.astype(jnp.bfloat16), "mdl", scatter_dimension=0, tiled=True
    ).astype(jnp.float32)
    return (resid_mine.astype(jnp.float32) + mlp_mine).astype(jnp.bfloat16)


def solution(mesh):
    return jax.shard_map(
        per_device,
        mesh=mesh,
        in_specs=(
            P("req", None),
            P(None, "mdl", None),
            P("mdl", None),
            P("mdl", None, None),
            P(None, "mdl", None),
            P(),
            P(),
            P(None, "req", "mdl"),
            P("req", None, "mdl", None),
            P("req"),
            P("req", None),
            P("req"),
            P(),
            P(),
            P(),
        ),
        out_specs=P(("req", "mdl"), None),
        check_vma=False,
    )
```

profile of v0, /device:TPU:8, one launch (start us, length us, event | category | flops | bytes accessed | tf_op | source)
XLA Modules:
  0.0 314.7 jit_solution(2396669354189061754)
XLA Ops:
  7.4 0.8 fusion.39
  8.6 0.8 mul.159
  9.5 0.8 mul.162
  10.9 6.5 %gather_fusion = bf16[64,2,224,128]{3,2,1,0:T(8,128)(2,1)} fusion(bf16[32,2,224,128]{3,2,1,0:T(8,128)(2,1)} %param.23, s32[1024]{0:T(1024)S(1)} %pad_clamp_fusion.1), kind=kCustom, calls=%fused_computation | custom fusion | bytes 14680320 | tf_op jit(solution)/shard_map/jit(_take)/gather | solution.py:100
  17.4 13.2 %convolution_convert_fusion.2 = bf16[64,64,2,224]{3,1,2,0:T(8,128)(2,1)} fusion(bf16[64,2,224,128]{3,2,1,0:T(8,128)(2,1)} %gather_fusion, s32[64,64]{1,0:T(8,128)S(1)} %iota_add_fusion), kind=kOutput, calls=%fused_computation.23 | convolution fusion | flops 472121344 | bytes 11026432 | tf_op jit(solution)/shard_map/skcr,srj->sjkc/dot_general | solution.py:107
  30.5 11.9 %all-to-all-start = ((bf16[32,2,64,2,224]{4,2,3,1,0:T(8,128)(2,1)}), bf16[32,2,64,2,224]{4,2,3,1,0:T(8,128)(2,1)}, u32[]{:S(2)}, u32[]{:S(2)}) async-start(bf16[32,2,64,2,224]{4,2,3,1,0:T(8,128)(2,1)} %bitcast.75), calls=%async_computation | async-start | bytes 8388608 | tf_op jit(solution)/shard_map/all_to_all | solution.py:111
  42.9 3.9 %fusion.19 = f32[3,768,224]{1,2,0:T(8,128)S(1)} fusion(bf16[3,224,1792]{2,1,0:T(8,128)(2,1)S(1)} %copy-done, bf16[768,1792]{1,0:T(8,128)(2,1)} %param.15), kind=kOutput, calls=%fused_computation.37 | convolution fusion | flops 1849688064 | bytes 7225344 | tf_op jit(solution)/shard_map/td,kcd->ktc/dot_general | solution.py:39
  46.8 1.3 copy-done.2
  48.3 2.8 fusion.55
  51.2 26.8 %psum.14 = bf16[768,16]{0,1:T(8,128)(2,1)S(1)} all-reduce(bf16[768,16]{0,1:T(8,128)(2,1)S(1)} %multiply_reduce_fusion), channel_id=1, replica_groups=mesh['req'=32,'mdl'=8] {'mdl'}, use_global_device_ids=true, to_apply=%region_4.5 | all-reduce | flops 12288 | bytes 49152 | tf_op jit(solution)/shard_map/psum | solution.py:54
  78.0 0.8 fusion.42
  78.9 0.8 fusion.41
  80.1 1.4 fusion.51
  81.6 0.9 fusion.56
  82.9 1.0 add_convert_fusion.3
  83.9 1.2 compare_and_fusion
  85.2 1.3 pad_add_fusion
  86.5 49.7 %all-to-all-done = bf16[32,2,64,2,224]{4,2,3,1,0:T(8,128)(2,1)} async-done(((bf16[32,2,64,2,224]{4,2,3,1,0:T(8,128)(2,1)}), bf16[32,2,64,2,224]{4,2,3,1,0:T(8,128)(2,1)}, u32[]{:S(2)}, u32[]{:S(2)}) %all-to-all-start) | async-done | bytes 3670048 | tf_op jit(solution)/shard_map/all_to_all | solution.py:111
  136.2 2.8 gather_fusion.1
  139.7 0.6 copy.30
  140.7 0.6 copy.29
  141.3 9.6 %fusion.54 = (f32[2,768]{1,0:T(2,128)S(1)}, f32[2,768,2304]{2,1,0:T(8,128)}) fusion(pred[768,2304]{1,0:T(8,128)(4,1)} %pad_add_fusion, bf16[768,2,112]{0,2,1:T(8,128)(2,1)S(1)} %copy-done.6, bf16[1536,2,112]{0,2,1:T(8,128)(2,1)S(1)} %copy.30, bf16[768,2,112]{0,2,1:T(8,128)(2,1)S(1)} %bitcast.83), kind=kOutput, calls=%fused_computation.97 | convolution fusion | flops 808945920 | bytes 17307648 | tf_op jit(solution)/shard_map/sub | solution.py:140
  150.9 7.6 %fusion.24 = bf16[2,112,768]{2,1,0:T(8,128)(2,1)S(1)} fusion(f32[2,768,2304]{2,1,0:T(8,128)} %get-tuple-element.20, f32[2,768]{1,0:T(2,128)S(1)} %get-tuple-element.19, bf16[1536,2,112]{0,2,1:T(8,128)(2,1)S(1)} %copy.29, bf16[768,2,112]{0,2,1:T(8,128)(2,1)S(1)} %copy-done.5), kind=kOutput, calls=%fused_computation.39 | convolution fusion | flops 802037760 | bytes 15538176 | tf_op jit(solution)/shard_map/hts,shd->thd/dot_general | solution.py:143
  158.4 2.5 convolution_convert_fusion
  161.1 0.5 all-gather.2.cloned.1.call-update
  161.9 71.7 %all-reduce.2.cloned.1.call-done = bf16[768,1792]{1,0:T(8,128)(2,1)} async-done(((bf16[768,1792]{1,0:T(8,128)(2,1)}), bf16[768,1792]{1,0:T(8,128)(2,1)}) %all-reduce.2.cloned.1.call-update) | async-done | bytes 2752528 | tf_op jit(solution)/shard_map/psum | solution.py:153
  233.6 5.3 %fusion.6 = (f32[768]{0:T(1024)S(1)}, bf16[768,1792]{1,0:T(8,128)(2,1)}) fusion(bf16[768,1792]{1,0:T(8,128)(2,1)} %all-reduce.2.cloned.1.call-done, bf16[768,1792]{1,0:T(8,128)(2,1)} %param.15), kind=kLoop, calls=%fused_computation.14 | loop fusion | flops 9633024 | bytes 8260608 | tf_op jit(solution)/shard_map/reduce_sum | solution.py:156
  238.9 14.1 %all-gather.2.cloned.1.call-done = bf16[3,1792,608]{2,1,0:T(8,128)(2,1)} async-done(((bf16[3,56,608]{2,1,0:T(8,128)(2,1)}), bf16[3,1792,608]{2,1,0:T(8,128)(2,1)}) %all-gather.2.cloned.1.call-update) | async-done | bytes 6537232 | tf_op jit(solution)/shard_map/all_gather | solution.py:159
  253.0 5.8 %fusion.16 = f32[768,608]{0,1:T(8,128)} fusion(bf16[3,1792,608]{2,1,0:T(8,128)(2,1)} %all-gather.2.cloned.1.call-done, bf16[768,1792]{1,0:T(8,128)(2,1)} %get-tuple-element.10, f32[1792]{0:T(1024)S(1)} %convert_element_type.123, f32[768]{0:T(1024)S(1)} %add_rsqrt_fusion), kind=kOutput, calls=%fused_computation.33 | convolution fusion | flops 1679032320 | bytes 6924288 | tf_op jit(solution)/shard_map/dot_general | solution.py:160
  258.9 10.5 %convolution_convert_fusion.1 = bf16[768,1792]{1,0:T(8,128)(2,1)} fusion(bf16[3,1792,608]{2,1,0:T(8,128)(2,1)} %all-gather.2.cloned.1.call-done, f32[768,608]{0,1:T(8,128)} %fusion.16, bf16[768,1792]{1,0:T(8,128)(2,1)} %get-tuple-element.10, f32[1792]{0:T(1024)S(1)} %convert_element_type.123, f32[768]{0:T(1024)S(1)} %add_rsqrt_fusion), kind=kOutput, calls=%fused_computation.20 | convolution fusion | flops 3356737536 | bytes 11970560 | tf_op jit(solution)/shard_map/tf,df->td/dot_general | solution.py:164
  269.4 36.0 %reduce-scatter.2.cloned.1.call-done = bf16[96,1792]{1,0:T(8,128)(2,1)} async-done(((bf16[768,1792]{1,0:T(8,128)(2,1)}), bf16[96,1792]{1,0:T(8,128)(2,1)}) %reduce-scatter.2.cloned.1.call-update) | async-done | bytes 344080 | tf_op jit(solution)/shard_map/reduce_scatter | solution.py:168
  305.4 1.9 add_convert_fusion.1
  (72 shorter events, 4.0 us)
Async XLA Ops:
  7.4 35.5 %copy-start = (bf16[3,224,1792]{2,1,0:T(8,128)(2,1)S(1)}, bf16[3,224,1792]{2,1,0:T(8,128)(2,1)}, u32[]{:S(2)}) copy-start(bf16[3,224,1792]{2,1,0:T(8,128)(2,1)} %param.16) | copy-start | bytes 7225348
  30.5 11.9 %copy-start.9 = (s32[1,24]{1,0:T(1,128)S(1)}, s32[1,24]{1,0:T(1,128)}, u32[]{:S(2)}) copy-start(s32[1,24]{1,0:T(1,128)} %param.25) | copy-start | bytes 292
  30.5 105.7 %all-to-all-start = ((bf16[32,2,64,2,224]{4,2,3,1,0:T(8,128)(2,1)}), bf16[32,2,64,2,224]{4,2,3,1,0:T(8,128)(2,1)}, u32[]{:S(2)}, u32[]{:S(2)}) async-start(bf16[32,2,64,2,224]{4,2,3,1,0:T(8,128)(2,1)} %bitcast.75), calls=%async_computation | async-start | bytes 8388608 | tf_op jit(solution)/shard_map/all_to_all | solution.py:111
  42.4 191.2 %all-reduce.2.cloned.1.call-start = ((), (), s32[]{:S(2)}) async-start(), calls=%async_computation.2 | async-start | bytes 5505024 | tf_op jit(solution)/shard_map/psum | solution.py:153
  42.9 5.3 %copy-start.7 = (s32[768]{0:T(1024)S(1)}, s32[768]{0:T(1024)}, u32[]{:S(2)}) copy-start(s32[768]{0:T(1024)} %param.24) | copy-start | bytes 9220
  42.9 5.4 %copy-start.4 = (bf16[8,1792,16]{1,2,0:T(8,128)(2,1)S(1)}, bf16[8,1792,16]{1,2,0:T(8,128)(2,1)}, u32[]{:S(2)}) copy-start(bf16[8,1792,16]{1,2,0:T(8,128)(2,1)} %param.18) | copy-start | bytes 1376260
  46.8 1.3 copy-start.2
  48.2 31.5 %copy-start.11 = (f32[4]{0:T(128)S(1)}, f32[4]{0:T(128)}, u32[]{:S(2)}) copy-start(f32[4]{0:T(128)} %param.20) | copy-start | bytes 52
  48.2 31.5 %copy-start.12 = (s32[24]{0:T(128)S(1)}, s32[24]{0:T(128)}, u32[]{:S(2)}) copy-start(s32[24]{0:T(128)} %param.26) | copy-start | bytes 292
  51.1 30.4 %copy-start.10 = (bf16[2,224,1024]{2,1,0:T(8,128)(2,1)S(1)}, bf16[2,224,1024]{2,1,0:T(8,128)(2,1)}, u32[]{:S(2)}) copy-start(bf16[2,224,1024]{2,1,0:T(8,128)(2,1)} %param.19) | copy-start | bytes 2752516
  139.6 1.6 copy-start.6
  141.3 9.6 %copy-start.5 = (bf16[768,2,112]{0,2,1:T(8,128)(2,1)S(1)}, bf16[768,2,112]{0,2,1:T(8,128)(2,1)}, u32[]{:S(2)}) copy-start(bf16[768,2,112]{0,2,1:T(8,128)(2,1)} %get-tuple-element.17) | copy-start | bytes 1032196
  150.9 7.6 %copy-start.3 = (bf16[224,1792]{1,0:T(8,128)(2,1)S(1)}, bf16[224,1792]{1,0:T(8,128)(2,1)}, u32[]{:S(2)}) copy-start(bf16[224,1792]{1,0:T(8,128)(2,1)} %param.17) | copy-start | bytes 2408452
  158.4 3.4 %copy-start.8 = (bf16[1792]{0:T(1024)(128)(2,1)S(1)}, bf16[1792]{0:T(1024)(128)(2,1)}, u32[]{:S(2)}) copy-start(bf16[1792]{0:T(1024)(128)(2,1)} %param.21) | copy-start | bytes 10756
  161.0 92.0 %all-gather.2.cloned.1.call-start = ((), (), s32[]{:S(2)}) async-start(), calls=%async_computation.3 | async-start | bytes 7096320 | tf_op jit(solution)/shard_map/all_gather | solution.py:159
  161.6 143.8 %reduce-scatter.2.cloned.1.call-start = ((), (), s32[]{:S(2)}) async-start(), calls=%async_computation.4 | async-start | bytes 3096576 | tf_op jit(solution)/shard_map/reduce_scatter | solution.py:168
  258.9 48.4 %copy-start.1 = (bf16[3,224,1792]{2,1,0:T(8,128)(2,1)S(1)}, bf16[3,224,1792]{2,1,0:T(8,128)(2,1)}, u32[]{:S(2)}) copy-start(bf16[3,224,1792]{2,1,0:T(8,128)(2,1)} %param.16) | copy-start | bytes 7225348
Sparse Core Ops, SparseCore 0:
  161.1 72.4 all-reduce.1
  269.5 35.7 reduce-scatter.1
Sparse Core Ops, SparseCore 1:
  164.5 88.5 all-gather.1
where the time goes:
time: 315 us
  waiting for transfers between devices  172 us (55%)
  matrix products  56.8 us (18%)
  blocking collectives  26.8 us (9%)
  local copies, waits for them, and re-layouts  17.7 us (6%)
  between operations  15.2 us (5%)
  other arithmetic  14 us (4%)
  starting transfers between devices  12.2 us (4%)
    psum x1, waiting for transfers between devices, per_device(): lax.psum(attn_part.astype(jnp.bfloat16), 'mdl').astype(jnp.float32)  71.7 us
    all_to_all x1, waiting for transfers between devices, per_device(): lax.all_to_all(source_pages, 'req', split_axis=0, concat_axis=0, tiled=True)  49.7 us
    reduce_scatter x1, waiting for transfers between devices, per_device(): lax.psum_scatter(mlp_part.astype(jnp.bfloat16), 'mdl', scatter_dimension=...  36 us
    psum x1, blocking collectives, per_device(): rank_feat = lax.psum(rank_part.astype(jnp.bfloat16), 'mdl')  26.8 us
    all_gather x1, waiting for transfers between devices, per_device(): full_mlp = lax.all_gather(feedforward_weight, 'req', axis=1, tiled=True)  14.1 us
    dot_general x1, matrix products, per_device(): jnp.einsum('skcr,srj->sjkc', pages, window_pick, preferred_element_type=j...  13.2 us
    all_to_all x1, starting transfers between devices, per_device(): lax.all_to_all(source_pages, 'req', split_axis=0, concat_axis=0, tiled=True)  11.9 us
    dot_general x1, matrix products, per_device(): jnp.einsum('tf,df->td', hidden, full_mlp[2], preferred_element_type=jnp.f...  10.5 us
  transfers between devices with their start and end apart: 4, of which 4 were waited for; matrix products, arithmetic and copies ran while one was open for 7% of the time, Pallas kernels for 0%

commit v1 on v0

--- a/solution.py
+++ b/solution.py
@@ -156,7 +156,10 @@
     mean_sq = jnp.mean(resid_wide * resid_wide, axis=1, keepdims=True)
     normed = (resid_wide * lax.rsqrt(mean_sq + 1e-06) * gain_wide).astype(jnp.bfloat16)
     resid_mine = lax.dynamic_slice_in_dim(resid_full, mdl_index * row_share, row_share, 0)
-    full_mlp = lax.all_gather(feedforward_weight, "req", axis=1, tiled=True)
+    size = lax.axis_size("req")
+    pieces = jnp.stack([feedforward_weight for _ in range(size)])
+    pieces = lax.all_to_all(pieces, "req", split_axis=0, concat_axis=0)
+    full_mlp = jnp.concatenate(pieces, axis=1)
     gate_part = jnp.dot(normed, full_mlp[0], preferred_element_type=jnp.float32)
     up_part = jnp.dot(normed, full_mlp[1], preferred_element_type=jnp.float32)
     hidden = (jax.nn.silu(gate_part) * up_part).astype(jnp.bfloat16)

time: 315 us -> 362 us (1.15)
  blocking collectives: 26.8 us -> 133 us
  waiting for transfers between devices: 172 us -> 115 us
  local copies, waits for them, and re-layouts: 17.7 us -> 27 us
  starting transfers between devices: 12.2 us -> 6.05 us
  matrix products: 56.8 us -> 52.9 us
    all_to_all x0 -> x1, blocking collectives: none -> 107 us  [per_device(): lax.all_to_all(source_pages, 'req', split_axis=0, concat_axis=0, tiled=True)]
    all_to_all x1, waiting for transfers between devices: 49.7 us -> 3.64 us  [per_device(): pieces = lax.all_to_all(pieces, 'req', split_axis=0, concat_axis=0)]
    all_gather x1 -> x0, waiting for transfers between devices: 14.1 us -> none  [per_device(): full_mlp = lax.all_gather(feedforward_weight, 'req', axis=1, tiled=True)]
    all_to_all x1, starting transfers between devices: 11.9 us -> 5.74 us  [per_device(): pieces = lax.all_to_all(pieces, 'req', split_axis=0, concat_axis=0)]
    slice x0 -> x1, local copies, waits for them, and re-layouts: none -> 5.91 us  [per_device(): up_part = jnp.dot(normed, full_mlp[1], preferred_element_type=jnp.float32)]
  transfers between devices with their start and end apart: 4 -> 3, of which waited for: 4 -> 3; matrix products, arithmetic and copies ran while one was open for 7% -> 13% of each run, Pallas kernels for 0% -> 0%
where the time goes in v1:
time: 362 us
  blocking collectives  133 us (37%)
  waiting for transfers between devices  115 us (32%)
  matrix products  52.9 us (15%)
  local copies, waits for them, and re-layouts  27 us (7%)
  other arithmetic  13.8 us (4%)
  between operations  13.8 us (4%)
  starting transfers between devices  6.05 us (2%)
    all_to_all x1, blocking collectives, per_device(): lax.all_to_all(source_pages, 'req', split_axis=0, concat_axis=0, tiled=True)  107 us
    psum x1, waiting for transfers between devices, per_device(): lax.psum(attn_part.astype(jnp.bfloat16), 'mdl').astype(jnp.float32)  72.9 us
    reduce_scatter x1, waiting for transfers between devices, per_device(): lax.psum_scatter(mlp_part.astype(jnp.bfloat16), 'mdl', scatter_dimension=...  38.9 us
    psum x1, blocking collectives, per_device(): rank_feat = lax.psum(rank_part.astype(jnp.bfloat16), 'mdl')  25.6 us
    dot_general x1, matrix products, per_device(): jnp.einsum('skcr,srj->sjkc', pages, window_pick, preferred_element_type=j...  11.7 us
    dot_general x1, matrix products, per_device(): jnp.einsum('tf,df->td', hidden, full_mlp[2], preferred_element_type=jnp.f...  10.6 us
    sub x1, matrix products, per_device(): exp_scores = jnp.exp(masked - row_max)  9.56 us
    dot_general x1, matrix products, per_device(): jnp.einsum('hts,shd->thd', weights, value_heads, preferred_element_type=j...  7.56 us
  transfers between devices with their start and end apart: 3, of which 3 were waited for; matrix products, arithmetic and copies ran while one was open for 13% of the time, Pallas kernels for 0%

profile of v1, /device:TPU:8, one launch (start us, length us, event | category | flops | bytes accessed | tf_op | source)
XLA Modules:
  0.0 361.8 jit_solution(2476705083671823541)
XLA Ops:
  6.5 0.8 fusion.38
  7.8 0.8 mul.159
  8.7 0.8 mul.162
  10.0 6.5 %gather_fusion = bf16[64,2,224,128]{3,2,1,0:T(8,128)(2,1)} fusion(bf16[32,2,224,128]{3,2,1,0:T(8,128)(2,1)} %param.23, s32[1024]{0:T(1024)S(1)} %pad_clamp_fusion.1), kind=kCustom, calls=%fused_computation | custom fusion | bytes 14680320 | tf_op jit(solution)/shard_map/jit(_take)/gather | solution.py:100
  16.5 11.7 %convolution_convert_fusion.2 = bf16[64,64,2,224]{3,1,2,0:T(8,128)(2,1)S(1)} fusion(bf16[64,2,224,128]{3,2,1,0:T(8,128)(2,1)} %gather_fusion, s32[64,64]{1,0:T(8,128)S(1)} %iota_add_fusion), kind=kOutput, calls=%fused_computation.23 | convolution fusion | flops 472121344 | bytes 11026432 | tf_op jit(solution)/shard_map/skcr,srj->sjkc/dot_general | solution.py:107
  28.3 107.2 %all_to_all.10 = bf16[32,2,64,2,224]{4,2,3,1,0:T(8,128)(2,1)} all-to-all(bf16[32,2,64,2,224]{4,2,3,1,0:T(8,128)(2,1)S(1)} %bitcast.69), channel_id=1, replica_groups=mesh['req'=32,'mdl'=8] {'req'}, dimensions={0} | all-to-all | bytes 7340032 | tf_op jit(solution)/shard_map/all_to_all | solution.py:111
  135.5 3.4 stack.2
  138.9 5.7 %all-to-all-start.1 = ((bf16[32,3,56,608]{3,2,1,0:T(8,128)(2,1)}), bf16[32,3,56,608]{3,2,1,0:T(8,128)(2,1)}, u32[]{:S(2)}, u32[]{:S(2)}) async-start(bf16[32,3,56,608]{3,2,1,0:T(8,128)(2,1)} %stack.2), calls=%async_computation.1 | async-start | bytes 13762560 | tf_op jit(solution)/shard_map/all_to_all | solution.py:161
  145.1 3.9 %fusion.17 = f32[3,768,224]{1,2,0:T(8,128)S(1)} fusion(bf16[3,224,1792]{2,1,0:T(8,128)(2,1)S(1)} %copy-done, bf16[768,1792]{1,0:T(8,128)(2,1)} %param.15), kind=kOutput, calls=%fused_computation.32 | convolution fusion | flops 1849688064 | bytes 7225344 | tf_op jit(solution)/shard_map/td,kcd->ktc/dot_general | solution.py:39
  149.0 1.3 copy-done.3
  150.5 2.8 fusion.55
  153.4 25.6 %psum.14 = bf16[768,16]{0,1:T(8,128)(2,1)S(1)} all-reduce(bf16[768,16]{0,1:T(8,128)(2,1)S(1)} %multiply_reduce_fusion), channel_id=1, replica_groups=mesh['req'=32,'mdl'=8] {'mdl'}, use_global_device_ids=true, to_apply=%region_4.5 | all-reduce | flops 12288 | bytes 49152 | tf_op jit(solution)/shard_map/psum | solution.py:54
  179.0 0.8 fusion.41
  179.9 0.8 fusion.40
  181.1 1.4 fusion.51
  182.6 0.9 fusion.56
  183.9 1.0 add_convert_fusion.3
  184.9 1.2 compare_and_fusion
  186.2 1.4 pad_add_fusion
  187.5 2.8 gather_fusion.1
  191.0 0.6 copy.30
  192.6 9.6 %fusion.54 = (f32[2,768]{1,0:T(2,128)S(1)}, f32[2,768,2304]{2,1,0:T(8,128)}) fusion(pred[768,2304]{1,0:T(8,128)(4,1)} %pad_add_fusion, bf16[768,2,112]{0,2,1:T(8,128)(2,1)S(1)} %copy-done.7, bf16[1536,2,112]{0,2,1:T(8,128)(2,1)S(1)} %copy.30, bf16[768,2,112]{0,2,1:T(8,128)(2,1)S(1)} %bitcast.81), kind=kOutput, calls=%fused_computation.93 | convolution fusion | flops 808945920 | bytes 17307648 | tf_op jit(solution)/shard_map/sub | solution.py:140
  202.2 7.6 %fusion.22 = bf16[2,112,768]{2,1,0:T(8,128)(2,1)S(1)} fusion(f32[2,768,2304]{2,1,0:T(8,128)} %get-tuple-element.23, f32[2,768]{1,0:T(2,128)S(1)} %get-tuple-element.22, bf16[1536,2,112]{0,2,1:T(8,128)(2,1)S(1)} %copy.29, bf16[768,2,112]{0,2,1:T(8,128)(2,1)S(1)} %copy-done.6), kind=kOutput, calls=%fused_computation.34 | convolution fusion | flops 802037760 | bytes 15538176 | tf_op jit(solution)/shard_map/hts,shd->thd/dot_general | solution.py:143
  209.8 2.5 convolution_convert_fusion
  212.6 72.9 %all-reduce.2.cloned.1.call-done = bf16[768,1792]{1,0:T(8,128)(2,1)} async-done(((bf16[768,1792]{1,0:T(8,128)(2,1)}), bf16[768,1792]{1,0:T(8,128)(2,1)}) %all-reduce.2.cloned.1.call-update) | async-done | bytes 2752528 | tf_op jit(solution)/shard_map/psum | solution.py:153
  285.5 5.1 %fusion.6 = (f32[768]{0:T(1024)S(1)}, bf16[768,1792]{1,0:T(8,128)(2,1)}) fusion(bf16[768,1792]{1,0:T(8,128)(2,1)} %all-reduce.2.cloned.1.call-done, bf16[768,1792]{1,0:T(8,128)(2,1)} %param.15), kind=kLoop, calls=%fused_computation.14 | loop fusion | flops 9633024 | bytes 8260608 | tf_op jit(solution)/shard_map/reduce_sum | solution.py:156
  290.6 3.6 %all-to-all-done.1 = bf16[32,3,56,608]{3,2,1,0:T(8,128)(2,1)} async-done(((bf16[32,3,56,608]{3,2,1,0:T(8,128)(2,1)}), bf16[32,3,56,608]{3,2,1,0:T(8,128)(2,1)}, u32[]{:S(2)}, u32[]{:S(2)}) %all-to-all-start.1) | async-done | bytes 6537248 | tf_op jit(solution)/shard_map/all_to_all | solution.py:161
  294.3 5.9 %fusion.50 = (bf16[1,32,56,608]{3,2,0,1:T(8,128)(2,1)}, bf16[1,32,56,608]{3,2,0,1:T(8,128)(2,1)}, bf16[1,32,56,608]{3,2,0,1:T(8,128)(2,1)S(1)}) fusion(bf16[3,32,56,608]{3,2,0,1:T(8,128)(2,1)} %bitcast.23), kind=kLoop, calls=%fused_computation.89 | loop fusion | bytes 13074432 | tf_op jit(solution)/shard_map/slice | solution.py:164
  300.2 3.4 fusion.28
  303.6 10.6 %convolution_convert_fusion.1 = bf16[768,1792]{1,0:T(8,128)(2,1)} fusion(bf16[1792,608]{1,0:T(8,128)(2,1)} %bitcast.76, f32[768,608]{0,1:T(8,128)} %fusion.28, bf16[1792,608]{1,0:T(8,128)(2,1)} %bitcast.75, bf16[768,1792]{1,0:T(8,128)(2,1)} %get-tuple-element.10, f32[1792]{0:T(1024)S(1)} %convert_element_type.123, f32[768]{0:T(1024)S(1)} %add_rsqrt_fusion), kind=kOutput, calls=%fused_computation.20 | convolution fusion | flops 3356737536 | bytes 11741184 | tf_op jit(solution)/shard_map/tf,df->td/dot_general | solution.py:167
  314.2 38.9 %reduce-scatter.2.cloned.1.call-done = bf16[96,1792]{1,0:T(8,128)(2,1)} async-done(((bf16[768,1792]{1,0:T(8,128)(2,1)}), bf16[96,1792]{1,0:T(8,128)(2,1)}) %reduce-scatter.2.cloned.1.call-update) | async-done | bytes 344080 | tf_op jit(solution)/shard_map/reduce_scatter | solution.py:171
  353.1 1.9 add_convert_fusion.1
  (76 shorter events, 4.6 us)
Async XLA Ops:
  6.5 138.6 %copy-start = (bf16[3,224,1792]{2,1,0:T(8,128)(2,1)S(1)}, bf16[3,224,1792]{2,1,0:T(8,128)(2,1)}, u32[]{:S(2)}) copy-start(bf16[3,224,1792]{2,1,0:T(8,128)(2,1)} %param.16) | copy-start | bytes 7225348
  28.3 107.2 %copy-start.8 = (bf16[3,56,608]{2,1,0:T(8,128)(2,1)S(1)}, bf16[3,56,608]{2,1,0:T(8,128)(2,1)}, u32[]{:S(2)}) copy-start(bf16[3,56,608]{2,1,0:T(8,128)(2,1)} %param.22) | copy-start | bytes 612868
  138.9 5.8 %copy-start.11 = (s32[1,24]{1,0:T(1,128)S(1)}, s32[1,24]{1,0:T(1,128)}, u32[]{:S(2)}) copy-start(s32[1,24]{1,0:T(1,128)} %param.25) | copy-start | bytes 292
  138.9 155.4 %all-to-all-start.1 = ((bf16[32,3,56,608]{3,2,1,0:T(8,128)(2,1)}), bf16[32,3,56,608]{3,2,1,0:T(8,128)(2,1)}, u32[]{:S(2)}, u32[]{:S(2)}) async-start(bf16[32,3,56,608]{3,2,1,0:T(8,128)(2,1)} %stack.2), calls=%async_computation.1 | async-start | bytes 13762560 | tf_op jit(solution)/shard_map/all_to_all | solution.py:161
  144.7 140.8 %all-reduce.2.cloned.1.call-start = ((), (), s32[]{:S(2)}) async-start(), calls=%async_computation.3 | async-start | bytes 5505024 | tf_op jit(solution)/shard_map/psum | solution.py:153
  145.1 5.3 %copy-start.9 = (s32[768]{0:T(1024)S(1)}, s32[768]{0:T(1024)}, u32[]{:S(2)}) copy-start(s32[768]{0:T(1024)} %param.24) | copy-start | bytes 9220
  145.1 5.4 %copy-start.5 = (bf16[8,1792,16]{1,2,0:T(8,128)(2,1)S(1)}, bf16[8,1792,16]{1,2,0:T(8,128)(2,1)}, u32[]{:S(2)}) copy-start(bf16[8,1792,16]{1,2,0:T(8,128)(2,1)} %param.18) | copy-start | bytes 1376260
  149.0 1.3 copy-start.3
  150.4 30.3 %copy-start.13 = (f32[4]{0:T(128)S(1)}, f32[4]{0:T(128)}, u32[]{:S(2)}) copy-start(f32[4]{0:T(128)} %param.20) | copy-start | bytes 52
  150.4 30.3 %copy-start.14 = (s32[24]{0:T(128)S(1)}, s32[24]{0:T(128)}, u32[]{:S(2)}) copy-start(s32[24]{0:T(128)} %param.26) | copy-start | bytes 292
  153.3 29.2 %copy-start.12 = (bf16[2,224,1024]{2,1,0:T(8,128)(2,1)S(1)}, bf16[2,224,1024]{2,1,0:T(8,128)(2,1)}, u32[]{:S(2)}) copy-start(bf16[2,224,1024]{2,1,0:T(8,128)(2,1)} %param.19) | copy-start | bytes 2752516
  191.0 1.6 copy-start.7
  192.6 9.6 %copy-start.6 = (bf16[768,2,112]{0,2,1:T(8,128)(2,1)S(1)}, bf16[768,2,112]{0,2,1:T(8,128)(2,1)}, u32[]{:S(2)}) copy-start(bf16[768,2,112]{0,2,1:T(8,128)(2,1)} %get-tuple-element.20) | copy-start | bytes 1032196
  202.2 7.6 %copy-start.4 = (bf16[224,1792]{1,0:T(8,128)(2,1)S(1)}, bf16[224,1792]{1,0:T(8,128)(2,1)}, u32[]{:S(2)}) copy-start(bf16[224,1792]{1,0:T(8,128)(2,1)} %param.17) | copy-start | bytes 2408452
  209.8 2.8 copy-start.10
  212.3 140.8 %reduce-scatter.2.cloned.1.call-start = ((), (), s32[]{:S(2)}) async-start(), calls=%async_computation.4 | async-start | bytes 3096576 | tf_op jit(solution)/shard_map/reduce_scatter | solution.py:171
  294.3 5.9 %copy-start.2 = (bf16[768,1792]{1,0:T(8,128)(2,1)S(1)}, bf16[768,1792]{1,0:T(8,128)(2,1)}, u32[]{:S(2)}) copy-start(bf16[768,1792]{1,0:T(8,128)(2,1)} %get-tuple-element.10) | copy-start | bytes 8257540
  303.6 51.4 %copy-start.1 = (bf16[3,224,1792]{2,1,0:T(8,128)(2,1)S(1)}, bf16[3,224,1792]{2,1,0:T(8,128)(2,1)}, u32[]{:S(2)}) copy-start(bf16[3,224,1792]{2,1,0:T(8,128)(2,1)} %param.16) | copy-start | bytes 7225348
Sparse Core Ops, SparseCore 0:
  212.4 73.0 all-reduce.1
  314.3 38.7 reduce-scatter.1
